TPU v7x, 32 devices: a whole 2x2x4 slice. The times are simulated.
32 devices in a mesh: dp: 8 (over y, x, core), seq: 4 (over z).
Axes of the slice: x: 2, y: 2, z: 4, core: 2. Of those that a mesh axis runs over, the one named last changes fastest.
Arguments:
- inputs: bfloat16 [32, 512, 1024], P('dp', 'seq'), may hold values from -6 to 6
- cotangent: bfloat16 [32, 512, 1024], P('dp', 'seq'), may hold values from -6 to 6
- lengths: int32 [32], P('dp'), may hold values from 80 to 512, as said below
- w_query: bfloat16 [1024, 1024], replicated, may hold values from -0.1875 to 0.1875
- b_query: float32 [1024], replicated, may hold values from -4 to 4
- w_key: bfloat16 [1024, 1024], replicated, may hold values from -0.1875 to 0.1875
- w_value: bfloat16 [1024, 1024], replicated, may hold values from -0.1875 to 0.1875
- b_value: float32 [1024], replicated, may hold values from -4 to 4
- w_output: bfloat16 [1024, 1024], replicated, may hold values from -0.75 to 0.75
- b_output: float32 [1024], replicated, may hold values from -4 to 4
- gain_first: float32 [1024], replicated, may hold values from 0.5 to 1.5
- shift_first: float32 [1024], replicated, may hold values from -4 to 4
- w_in: bfloat16 [1024, 4096], replicated, may hold values from -0.1875 to 0.1875
- b_in: float32 [4096], replicated, may hold values from -4 to 4
- w_out: bfloat16 [4096, 1024], replicated, may hold values from -0.1875 to 0.1875
- b_out: float32 [1024], replicated, may hold values from -4 to 4
- gain_second: float32 [1024], replicated, may hold values from 0.5 to 1.5
- shift_second: float32 [1024], replicated, may hold values from -4 to 4
Outputs:
- outputs: bfloat16 [32, 512, 1024], P('dp', 'seq')
- grad_inputs: float32 [32, 512, 1024], P('dp', 'seq')
- grad_w_query: float32 [1024, 1024], P(('dp', 'seq'))
- grad_b_query: float32 [1024], P(('dp', 'seq'))
- grad_w_key: float32 [1024, 1024], P(('dp', 'seq'))
- grad_w_value: float32 [1024, 1024], P(('dp', 'seq'))
- grad_b_value: float32 [1024], P(('dp', 'seq'))
- grad_w_output: float32 [1024, 1024], P(('dp', 'seq'))
- grad_b_output: float32 [1024], P(('dp', 'seq'))
- grad_gain_first: float32 [1024], P(('dp', 'seq'))
- grad_shift_first: float32 [1024], P(('dp', 'seq'))
- grad_w_in: float32 [1024, 4096], P(('dp', 'seq'))
- grad_b_in: float32 [4096], P(('dp', 'seq'))
- grad_w_out: float32 [4096, 1024], P(('dp', 'seq'))
- grad_b_out: float32 [1024], P(('dp', 'seq'))
- grad_gain_second: float32 [1024], P(('dp', 'seq'))
- grad_shift_second: float32 [1024], P(('dp', 'seq'))
Inputs may be any that keep to these rules, and one draw needn't show every extreme that they name: A page's real tokens are its first lengths slots. Some page is full and some page has exactly 80 real tokens.
All inputs are finite; a program needn't handle non-finite values.
Results may differ from a plain program's by a relative error of at most 0.015.
Values may be sent and summed in bfloat16 or wider, within the bound.
No kernel may reach another device: no remote copies, remote signals or barrier semaphores. Data moves between devices by JAX's collectives and lax.ppermute only.
A program may use at most 320 MiB of HBM per device.

v0:
```python
import math
import jax
import jax.numpy as jnp
from jax import lax
from jax.sharding import PartitionSpec as P

HEAD_DIM = 64
MICRO = 4
EPS = 1e-05


def dense(left, right):
    return jnp.dot(left, right, preferred_element_type=jnp.float32)


def dense_back(left, right):
    return lax.dot_general(
        left, right, (((1,), (1,)), ((), ())), preferred_element_type=jnp.float32
    )


def weight_term(left, right):
    return lax.dot_general(
        left, right, (((0,), (0,)), ((), ())), preferred_element_type=jnp.float32
    )


def norm_parts(summed):
    centred = summed - jnp.mean(summed, -1, keepdims=True)
    factor = lax.rsqrt(jnp.mean(centred * centred, -1, keepdims=True) + EPS)
    return (centred * factor, factor)


def norm_back(grad_normed, normed, factor):
    return factor * (
        grad_normed
        - jnp.mean(grad_normed, -1, keepdims=True)
        - normed * jnp.mean(grad_normed * normed, -1, keepdims=True)
    )


def gelu_slope(inner):
    cumulative = 0.5 * (1.0 + lax.erf(inner * 0.7071067811865476))
    density = jnp.exp(-0.5 * inner * inner) * 0.3989422804014327
    return cumulative + inner * density


def add_pairs(left, right):
    return tuple((first + second for first, second in zip(left, right)))


def on_device(
    inputs,
    cotangent,
    lengths,
    w_query,
    b_query,
    w_key,
    w_value,
    b_value,
    w_output,
    b_output,
    gain_first,
    shift_first,
    w_in,
    b_in,
    w_out,
    b_out,
    gain_second,
    shift_second,
):
    pages_dev, slots_dev, width = inputs.shape
    seq_count = lax.axis_size("seq")
    slots_all = slots_dev * seq_count
    head_size = HEAD_DIM
    local_width = width // seq_count
    heads_dev = local_width // head_size
    scale = 1.0 / math.sqrt(head_size)
    group = pages_dev // MICRO
    rows = group * slots_dev
    first_slot = lax.axis_index("seq") * slots_dev
    key_place = jnp.arange(slots_all, dtype=jnp.int32)
    row_place = first_slot + jnp.arange(slots_dev, dtype=jnp.int32)
    lower_shapes = (w_query.shape, b_query.shape, w_key.shape, w_value.shape, b_value.shape)
    upper_shapes = (
        w_output.shape,
        b_output.shape,
        gain_first.shape,
        shift_first.shape,
        w_in.shape,
        b_in.shape,
        w_out.shape,
        b_out.shape,
        gain_second.shape,
        shift_second.shape,
    )
    lower_totals = tuple((jnp.zeros(shape, jnp.float32) for shape in lower_shapes))
    upper_totals = tuple((jnp.zeros(shape, jnp.float32) for shape in upper_shapes))
    results = []
    input_grads = []
    for micro_step in range(MICRO):
        block = inputs[micro_step * group : (micro_step + 1) * group].reshape(rows, width)
        block_lengths = lengths[micro_step * group : (micro_step + 1) * group]
        queries = (dense(block, w_query) + b_query).astype(jnp.bfloat16)
        keys_local = dense(block, w_key).astype(jnp.bfloat16)
        values = (dense(block, w_value) + b_value).astype(jnp.bfloat16)
        packed = jnp.stack([queries, keys_local, values]).reshape(
            3, group, slots_dev, seq_count, local_width
        )
        spread = lax.all_to_all(packed, "seq", split_axis=3, concat_axis=2, tiled=True)
        head_q = spread[0].reshape(group, slots_all, heads_dev, head_size)
        head_k = spread[1].reshape(group, slots_all, heads_dev, head_size)
        head_v = spread[2].reshape(group, slots_all, heads_dev, head_size)
        key_live = key_place[None, :] < block_lengths[:, None]
        scores = (
            jnp.einsum("gqhd,gkhd->ghqk", head_q, head_k, preferred_element_type=jnp.float32)
            * scale
        )
        scores = jnp.where(key_live[:, None, None, :], scores, -1e30)
        largest = jnp.max(scores, -1, keepdims=True)
        expon = jnp.exp(scores - largest)
        totals_row = jnp.sum(expon, -1, keepdims=True)
        probs = expon / totals_row
        log_total = largest + jnp.log(totals_row)
        context = jnp.einsum(
            "ghqk,gkhd->gqhd",
            probs.astype(jnp.bfloat16),
            head_v,
            preferred_element_type=jnp.float32,
        ).astype(jnp.bfloat16)
        context = context.reshape(group, slots_all, 1, local_width)
        gathered = lax.all_to_all(context, "seq", split_axis=1, concat_axis=2, tiled=True).reshape(
            rows, width
        )
        attended = dense(gathered, w_output) + b_output
        normed_first, factor_first = norm_parts(block.astype(jnp.float32) + attended)
        hidden = normed_first * gain_first + shift_first
        hidden_low = hidden.astype(jnp.bfloat16)
        inner = dense(hidden_low, w_in) + b_in
        activated = jax.nn.gelu(inner, approximate=False).astype(jnp.bfloat16)
        branch = dense(activated, w_out) + b_out
        normed_second, factor_second = norm_parts(hidden + branch)
        result = normed_second * gain_second + shift_second
        results.append(result.astype(jnp.bfloat16).reshape(group, slots_dev, width))
        row_live = (
            (row_place[None, :] < block_lengths[:, None]).astype(jnp.float32).reshape(rows, 1)
        )
        upstream = (
            cotangent[micro_step * group : (micro_step + 1) * group]
            .reshape(rows, width)
            .astype(jnp.float32)
            * row_live
        )
        g_gain_second = jnp.sum(upstream * normed_second, 0)
        g_shift_second = jnp.sum(upstream, 0)
        d_second = norm_back(upstream * gain_second, normed_second, factor_second)
        d_branch = d_second.astype(jnp.bfloat16)
        g_w_out = weight_term(activated, d_branch)
        g_b_out = jnp.sum(d_branch.astype(jnp.float32), 0)
        d_inner = (dense_back(d_branch, w_out) * gelu_slope(inner)).astype(jnp.bfloat16)
        g_w_in = weight_term(hidden_low, d_inner)
        g_b_in = jnp.sum(d_inner.astype(jnp.float32), 0)
        d_hidden = d_second + dense_back(d_inner, w_in)
        g_gain_first = jnp.sum(d_hidden * normed_first, 0)
        g_shift_first = jnp.sum(d_hidden, 0)
        d_first = norm_back(d_hidden * gain_first, normed_first, factor_first)
        d_attended = d_first.astype(jnp.bfloat16)
        g_w_output = weight_term(gathered, d_attended)
        g_b_output = jnp.sum(d_attended.astype(jnp.float32), 0)
        upper_terms = (
            g_w_output,
            g_b_output,
            g_gain_first,
            g_shift_first,
            g_w_in,
            g_b_in,
            g_w_out,
            g_b_out,
            g_gain_second,
            g_shift_second,
        )
        d_context = dense_back(d_attended, w_output).astype(jnp.bfloat16)
        d_context = d_context.reshape(group, slots_dev, seq_count, local_width)
        head_grad = lax.all_to_all(d_context, "seq", split_axis=2, concat_axis=1, tiled=True)
        head_grad = head_grad.reshape(group, slots_all, heads_dev, head_size)
        scores_again = (
            jnp.einsum("gqhd,gkhd->ghqk", head_q, head_k, preferred_element_type=jnp.float32)
            * scale
        )
        scores_again = jnp.where(key_live[:, None, None, :], scores_again, -1e30)
        probs_again = jnp.exp(scores_again - log_total)
        d_probs = jnp.einsum(
            "gqhd,gkhd->ghqk", head_grad, head_v, preferred_element_type=jnp.float32
        )
        d_vals = jnp.einsum(
            "ghqk,gqhd->gkhd",
            probs_again.astype(jnp.bfloat16),
            head_grad,
            preferred_element_type=jnp.float32,
        )
        inner_sum = jnp.sum(probs_again * d_probs, -1, keepdims=True)
        d_scores = (probs_again * (d_probs - inner_sum)).astype(jnp.bfloat16)
        d_queries = (
            jnp.einsum("ghqk,gkhd->gqhd", d_scores, head_k, preferred_element_type=jnp.float32)
            * scale
        )
        d_keys = (
            jnp.einsum("ghqk,gqhd->gkhd", d_scores, head_q, preferred_element_type=jnp.float32)
            * scale
        )
        stacked = jnp.stack([d_queries, d_keys, d_vals]).astype(jnp.bfloat16)
        stacked = stacked.reshape(3, group, slots_all, 1, local_width)
        returned = lax.all_to_all(stacked, "seq", split_axis=2, concat_axis=3, tiled=True).reshape(
            3, rows, width
        )
        g_w_query = weight_term(block, returned[0])
        g_b_query = jnp.sum(returned[0].astype(jnp.float32), 0)
        g_w_key = weight_term(block, returned[1])
        g_w_value = weight_term(block, returned[2])
        g_b_value = jnp.sum(returned[2].astype(jnp.float32), 0)
        grad_block = (
            d_first
            + dense_back(returned[0], w_query)
            + dense_back(returned[1], w_key)
            + dense_back(returned[2], w_value)
        )
        input_grads.append(grad_block.reshape(group, slots_dev, width))
        lower_terms = (g_w_query, g_b_query, g_w_key, g_w_value, g_b_value)
        lower_totals = add_pairs(lower_totals, lower_terms)
        upper_totals = add_pairs(upper_totals, upper_terms)
    summed = lax.psum_scatter(
        lower_totals + upper_totals, ("dp", "seq"), scatter_dimension=0, tiled=True
    )
    lower_totals = tuple(summed[:5])
    upper_totals = tuple(summed[5:])
    return (
        jnp.concatenate(results, 0),
        jnp.concatenate(input_grads, 0),
        lower_totals[0],
        lower_totals[1],
        lower_totals[2],
        lower_totals[3],
        lower_totals[4],
        upper_totals[0],
        upper_totals[1],
        upper_totals[2],
        upper_totals[3],
        upper_totals[4],
        upper_totals[5],
        upper_totals[6],
        upper_totals[7],
        upper_totals[8],
        upper_totals[9],
    )


def solution(mesh):
    in_specs = (
        P("dp", "seq", None),
        P("dp", "seq", None),
        P("dp"),
        P(),
        P(),
        P(),
        P(),
        P(),
        P(),
        P(),
        P(),
        P(),
        P(),
        P(),
        P(),
        P(),
        P(),
        P(),
    )
    out_specs = (
        P("dp", "seq", None),
        P("dp", "seq", None),
        P(("dp", "seq"), None),
        P(("dp", "seq")),
        P(("dp", "seq"), None),
        P(("dp", "seq"), None),
        P(("dp", "seq")),
        P(("dp", "seq"), None),
        P(("dp", "seq")),
        P(("dp", "seq")),
        P(("dp", "seq")),
        P(("dp", "seq"), None),
        P(("dp", "seq")),
        P(("dp", "seq"), None),
        P(("dp", "seq")),
        P(("dp", "seq")),
        P(("dp", "seq")),
    )
    return jax.shard_map(
        on_device, mesh=mesh, in_specs=in_specs, out_specs=out_specs, check_vma=False
    )
```

profile of v0, /device:TPU:0, one launch (start us, length us, event | category | flops | bytes accessed | tf_op | source)
XLA Modules:
  0.0 1803.7 jit_solution(12697095188819701354)
XLA Ops:
  22.5 6.3 all-to-all-start.6
  222.2 5.4 convolution_add_fusion.3
  227.7 6.3 fusion.292
  234.0 5.5 all-to-all-start.5
  245.2 5.4 convolution_add_fusion.2
  250.7 5.6 fusion.289
  273.6 9.7 fusion.298
  293.7 9.1 fusion.295
  307.5 7.4 convert_reduce_fusion.3
  315.0 7.5 convert_reduce_fusion
  323.3 8.1 convert_reduce_fusion.1
  334.3 7.5 convert_reduce_fusion.2
  382.9 7.4 add_add_fusion.2
  431.0 5.4 all-to-all-start.10
  466.4 27.6 %all-to-all-done.9 = bf16[3,1,512,1,256]{4,0,3,1,2:T(4,128)(2,1)} async-done(((bf16[3,1,512,1,256]{4,0,3,1,2:T(4,128)(2,1)}), bf16[3,1,512,1,256]{4,0,3,1,2:T(4,128)(2,1)}, u32[]{:S(2)}, u32[]{:S(2)}) %all-to-all-start.9) | async-done | bytes 786464 | tf_op jit(solution)/shard_map/all_to_all | solution.py:213
  522.2 16.7 all-to-all-done.13
  557.7 17.1 all-to-all-done.15
  587.9 16.9 all-to-all-done.11
  625.0 5.4 copy.277
  644.0 9.7 fusion.252
  653.7 9.8 fusion.246
  663.5 9.7 fusion.240
  673.2 24.1 %add_add_fusion = f32[4096,1024]{1,0:T(8,128)} fusion(f32[4096,1024]{1,0:T(8,128)} %fusion.240, f32[4096,1024]{1,0:T(8,128)} %fusion.252, f32[4096,1024]{1,0:T(8,128)} %fusion.246, f32[128,1024]{1,0:T(8,128)S(1)} %copy-done.40, f32[128,4096]{1,0:T(8,128)S(1)} %copy-done.25), kind=kOutput, calls=%fused_computation | convolution fusion | flops 1120534528 | bytes 69730304 | tf_op jit(solution)/shard_map/dot_general | solution.py:23
  698.4 9.4 fusion.257
  707.9 8.2 fusion.260
  716.1 8.2 fusion.263
  724.3 23.2 %add_add_fusion.1 = f32[1024,4096]{1,0:T(8,128)} fusion(f32[1024,4096]{1,0:T(8,128)} %fusion.257, f32[1024,4096]{1,0:T(8,128)} %fusion.263, f32[1024,4096]{1,0:T(8,128)} %fusion.260, bf16[128,4096]{1,0:T(8,128)(2,1)S(1)} %copy-done.49, f32[128,1024]{1,0:T(8,128)S(1)} %copy-done.14, f32[128]{0:T(128)S(1)} %copy-done.181, f32[128]{0:T(128)S(1)} %copy-done.149, ...), kind=kOutput, calls=%fused_computation.1 | convolution fusion | flops 1086980096 | bytes 68690944 | tf_op jit(solution)/shard_map/dot_general | solution.py:23
  756.1 39.9 %all-reduce.9 = (f32[1024]{0:T(1024)S(1)}, f32[1024]{0:T(1024)S(1)}, f32[1024]{0:T(1024)S(1)}, f32[1024]{0:T(1024)S(1)}, f32[1024]{0:T(1024)S(1)}, /*index=5*/f3...) all-reduce(f32[1024]{0:T(1024)S(1)} %bitcast.508, ...), channel_id=3, replica_groups=mesh['dp'=8,'seq'=4] {'dp','seq'}, use_global_device_ids=true, to_apply=%region_49.50.clone | all-reduce | flops 12288 | bytes 98304
  816.2 101.8 %reduce-scatter.21.cloned.1.call-done = f32[32,1024]{1,0:T(8,128)} async-done(((f32[1024,1024]{1,0:T(8,128)}), f32[32,1024]{1,0:T(8,128)}) %reduce-scatter.21.cloned.1.call-update) | async-done | bytes 131088
  918.0 151.7 %reduce-scatter.19.cloned.1.call-done = f32[32,1024]{1,0:T(8,128)} async-done(((f32[1024,1024]{1,0:T(8,128)}), f32[32,1024]{1,0:T(8,128)}) %reduce-scatter.19.cloned.1.call-update) | async-done | bytes 131088
  1069.7 362.3 %reduce-scatter.17.cloned.1.call-done = f32[128,1024]{1,0:T(8,128)} async-done(((f32[4096,1024]{1,0:T(8,128)}), f32[128,1024]{1,0:T(8,128)}) %reduce-scatter.17.cloned.1.call-update) | async-done | bytes 524304 | tf_op jit(solution)/shard_map/reduce_scatter | solution.py:231
  1432.0 364.7 %reduce-scatter.15.cloned.1.call-done = f32[32,4096]{1,0:T(8,128)} async-done(((f32[1024,4096]{1,0:T(8,128)}), f32[32,4096]{1,0:T(8,128)}) %reduce-scatter.15.cloned.1.call-update) | async-done | bytes 524304 | tf_op jit(solution)/shard_map/reduce_scatter | solution.py:231
  (726 shorter events, 483.5 us)
Async XLA Ops:
  7.2 214.1 %copy-start = (bf16[1024,1024]{1,0:T(8,128)(2,1)S(1)}, bf16[1024,1024]{1,0:T(8,128)(2,1)}, u32[]{:S(2)}) copy-start(bf16[1024,1024]{1,0:T(8,128)(2,1)} %param.26) | copy-start | bytes 6291460
  22.5 26.6 %all-to-all-start.6 = ((bf16[3,1,128,4,256]{4,2,1,0,3:T(8,128)(2,1)}), bf16[3,1,128,4,256]{4,2,1,0,3:T(8,128)(2,1)}, u32[]{:S(2)}, u32[]{:S(2)}) async-start(bf16[3,1,128,4,256]{4,2,1,0,3:T(8,128)(2,1)} %pad_maximum_fusion.9), calls=%async_computation.6 | async-start | bytes 1572864 | tf_op jit(solution)/shard_map/all_to_all | solution.py:110
  49.1 23.9 %all-to-all-start.4 = ((bf16[3,1,128,4,256]{4,2,1,0,3:T(8,128)(2,1)}), bf16[3,1,128,4,256]{4,2,1,0,3:T(8,128)(2,1)}, u32[]{:S(2)}, u32[]{:S(2)}) async-start(bf16[3,1,128,4,256]{4,2,1,0,3:T(8,128)(2,1)} %pad_maximum_fusion.8), calls=%async_computation.4 | async-start | bytes 1572864 | tf_op jit(solution)/shard_map/all_to_all | solution.py:110
  73.0 23.9 %all-to-all-start.2 = ((bf16[3,1,128,4,256]{4,2,1,0,3:T(8,128)(2,1)}), bf16[3,1,128,4,256]{4,2,1,0,3:T(8,128)(2,1)}, u32[]{:S(2)}, u32[]{:S(2)}) async-start(bf16[3,1,128,4,256]{4,2,1,0,3:T(8,128)(2,1)} %pad_maximum_fusion.7), calls=%async_computation.2 | async-start | bytes 1572864 | tf_op jit(solution)/shard_map/all_to_all | solution.py:110
  96.9 45.7 %all-to-all-start = ((bf16[3,1,128,4,256]{4,2,1,0,3:T(8,128)(2,1)}), bf16[3,1,128,4,256]{4,2,1,0,3:T(8,128)(2,1)}, u32[]{:S(2)}, u32[]{:S(2)}) async-start(bf16[3,1,128,4,256]{4,2,1,0,3:T(8,128)(2,1)} %pad_maximum_fusion.6), calls=%async_computation | async-start | bytes 1572864 | tf_op jit(solution)/shard_map/all_to_all | solution.py:110
  110.0 90.2 %copy-start.65 = (bf16[512,4,64]{0,2,1:T(8,128)(2,1)}, bf16[512,4,64]{0,2,1:T(8,128)(2,1)S(1)}, u32[]{:S(2)}) copy-start(bf16[512,4,64]{0,2,1:T(8,128)(2,1)S(1)} %reshape.1119) | copy-start | bytes 786436
  168.9 42.3 %all-to-all-start.1 = ((bf16[4,2,16384]{2,1,0:T(2,128)(2,1)}), bf16[4,2,16384]{2,1,0:T(2,128)(2,1)}, u32[]{:S(2)}, u32[]{:S(2)}) async-start(bf16[4,2,16384]{2,1,0:T(2,128)(2,1)} %reshape.1151), calls=%async_computation.1 | async-start | bytes 524288 | tf_op jit(solution)/shard_map/all_to_all | solution.py:132
  211.2 22.9 %all-to-all-start.3 = ((bf16[4,2,16384]{2,1,0:T(2,128)(2,1)}), bf16[4,2,16384]{2,1,0:T(2,128)(2,1)}, u32[]{:S(2)}, u32[]{:S(2)}) async-start(bf16[4,2,16384]{2,1,0:T(2,128)(2,1)} %reshape.1149), calls=%async_computation.3 | async-start | bytes 524288 | tf_op jit(solution)/shard_map/all_to_all | solution.py:132
  221.9 126.5 %copy-start.142 = (f32[128]{0:T(128)}, f32[128]{0:T(128)S(1)}, u32[]{:S(2)}) copy-start(f32[128]{0:T(128)S(1)} %broadcast_multiply_fusion.23) | copy-start | bytes 1540
  222.2 126.3 %copy-start.150 = (f32[128]{0:T(128)}, f32[128]{0:T(128)S(1)}, u32[]{:S(2)}) copy-start(f32[128]{0:T(128)S(1)} %add_rsqrt_fusion.7) | copy-start | bytes 1540
  234.0 23.9 %all-to-all-start.5 = ((bf16[4,2,16384]{2,1,0:T(2,128)(2,1)}), bf16[4,2,16384]{2,1,0:T(2,128)(2,1)}, u32[]{:S(2)}, u32[]{:S(2)}) async-start(bf16[4,2,16384]{2,1,0:T(2,128)(2,1)} %reshape.1147), calls=%async_computation.5 | async-start | bytes 524288 | tf_op jit(solution)/shard_map/all_to_all | solution.py:132
  244.9 111.5 %copy-start.144 = (f32[128]{0:T(128)}, f32[128]{0:T(128)S(1)}, u32[]{:S(2)}) copy-start(f32[128]{0:T(128)S(1)} %broadcast_multiply_fusion.21) | copy-start | bytes 1540
  245.1 111.3 %copy-start.152 = (f32[128]{0:T(128)}, f32[128]{0:T(128)S(1)}, u32[]{:S(2)}) copy-start(f32[128]{0:T(128)S(1)} %add_rsqrt_fusion.5) | copy-start | bytes 1540
  257.9 25.3 %all-to-all-start.7 = ((bf16[4,2,16384]{2,1,0:T(2,128)(2,1)}), bf16[4,2,16384]{2,1,0:T(2,128)(2,1)}, u32[]{:S(2)}, u32[]{:S(2)}) async-start(bf16[4,2,16384]{2,1,0:T(2,128)(2,1)} %reshape.1145), calls=%async_computation.7 | async-start | bytes 524288 | tf_op jit(solution)/shard_map/all_to_all | solution.py:132
  268.6 87.9 %copy-start.146 = (f32[128]{0:T(128)}, f32[128]{0:T(128)S(1)}, u32[]{:S(2)}) copy-start(f32[128]{0:T(128)S(1)} %broadcast_multiply_fusion.19) | copy-start | bytes 1540
  268.8 87.7 %copy-start.154 = (f32[128]{0:T(128)}, f32[128]{0:T(128)S(1)}, u32[]{:S(2)}) copy-start(f32[128]{0:T(128)S(1)} %add_rsqrt_fusion.3) | copy-start | bytes 1540
  288.6 67.8 %copy-start.13 = (f32[128,1024]{1,0:T(8,128)}, f32[128,1024]{1,0:T(8,128)S(1)}, u32[]{:S(2)}) copy-start(f32[128,1024]{1,0:T(8,128)S(1)} %get-tuple-element.229) | copy-start | bytes 1572868
  377.8 12.5 all-to-all-start.8
  382.9 433.3 %reduce-scatter.13.cloned.1.call-start = ((), (), s32[]{:S(2)}) async-start(), calls=%async_computation.22 | async-start | bytes 4325376 | tf_op jit(solution)/shard_map/reduce_scatter | solution.py:231
  390.4 15.6 all-to-all-start.12
  406.0 25.0 %all-to-all-start.14 = ((bf16[1,128,4,256]{3,1,0,2:T(8,128)(2,1)}), bf16[1,128,4,256]{3,1,0,2:T(8,128)(2,1)}, u32[]{:S(2)}, u32[]{:S(2)}) async-start(bf16[1,128,4,256]{3,1,0,2:T(8,128)(2,1)} %copy.244), calls=%async_computation.14 | async-start | bytes 524288 | tf_op jit(solution)/shard_map/all_to_all | solution.py:184
  431.0 17.9 all-to-all-start.10
  448.9 45.1 %all-to-all-start.9 = ((bf16[3,1,512,1,256]{4,0,3,1,2:T(4,128)(2,1)}), bf16[3,1,512,1,256]{4,0,3,1,2:T(4,128)(2,1)}, u32[]{:S(2)}, u32[]{:S(2)}) async-start(bf16[3,1,512,1,256]{4,0,3,1,2:T(4,128)(2,1)} %pad_maximum_fusion.2), calls=%async_computation.9 | async-start | bytes 2097152 | tf_op jit(solution)/shard_map/all_to_all | solution.py:213
  494.0 44.9 %all-to-all-start.13 = ((bf16[3,1,512,1,256]{4,0,3,1,2:T(4,128)(2,1)}), bf16[3,1,512,1,256]{4,0,3,1,2:T(4,128)(2,1)}, u32[]{:S(2)}, u32[]{:S(2)}) async-start(bf16[3,1,512,1,256]{4,0,3,1,2:T(4,128)(2,1)} %pad_maximum_fusion.4), calls=%async_computation.13 | async-start | bytes 2097152 | tf_op jit(solution)/shard_map/all_to_all | solution.py:213
  538.9 36.0 %all-to-all-start.15 = ((bf16[3,1,512,1,256]{4,0,3,1,2:T(4,128)(2,1)}), bf16[3,1,512,1,256]{4,0,3,1,2:T(4,128)(2,1)}, u32[]{:S(2)}, u32[]{:S(2)}) async-start(bf16[3,1,512,1,256]{4,0,3,1,2:T(4,128)(2,1)} %pad_maximum_fusion.5), calls=%async_computation.15 | async-start | bytes 2097152 | tf_op jit(solution)/shard_map/all_to_all | solution.py:213
  574.9 29.9 %all-to-all-start.11 = ((bf16[3,1,512,1,256]{4,0,3,1,2:T(4,128)(2,1)}), bf16[3,1,512,1,256]{4,0,3,1,2:T(4,128)(2,1)}, u32[]{:S(2)}, u32[]{:S(2)}) async-start(bf16[3,1,512,1,256]{4,0,3,1,2:T(4,128)(2,1)} %pad_maximum_fusion.3), calls=%async_computation.11 | async-start | bytes 2097152 | tf_op jit(solution)/shard_map/all_to_all | solution.py:213
  579.1 237.1 %reduce-scatter.23.cloned.1.call-start = ((), (), s32[]{:S(2)}) async-start(), calls=%async_computation.27 | async-start | bytes 4325376
  618.5 299.5 %reduce-scatter.21.cloned.1.call-start = ((), (), s32[]{:S(2)}) async-start(), calls=%async_computation.26 | async-start | bytes 4325376
  630.4 439.3 %reduce-scatter.19.cloned.1.call-start = ((), (), s32[]{:S(2)}) async-start(), calls=%async_computation.25 | async-start | bytes 4325376
  642.3 789.7 %reduce-scatter.17.cloned.1.call-start = ((), (), s32[]{:S(2)}) async-start(), calls=%async_computation.24 | async-start | bytes 17301504 | tf_op jit(solution)/shard_map/reduce_scatter | solution.py:231
  697.4 1099.2 %reduce-scatter.15.cloned.1.call-start = ((), (), s32[]{:S(2)}) async-start(), calls=%async_computation.23 | async-start | bytes 17301504 | tf_op jit(solution)/shard_map/reduce_scatter | solution.py:231
  813.8 982.8 %copy-start.1 = (bf16[1024,1024]{1,0:T(8,128)(2,1)S(1)}, bf16[1024,1024]{1,0:T(8,128)(2,1)}, u32[]{:S(2)}) copy-start(bf16[1024,1024]{1,0:T(8,128)(2,1)} %param.26) | copy-start | bytes 6291460
  (182 other events, 1405.0 us)
Sparse Core Ops, SparseCore 0:
  390.5 174.6 reduce-scatter.12
  618.6 148.8 reduce-scatter.22
  770.3 147.6 reduce-scatter.20
  920.7 148.9 reduce-scatter.18
  1072.4 359.5 reduce-scatter.16
  1434.7 361.8 reduce-scatter.14
where the time goes:
time: 1820 us; the launch traced here: 1800 us
  waiting for transfers between devices  1080 us (59%)
  matrix products  324 us (18%)
  local copies, waits for them, and re-layouts  188 us (10%)
  other arithmetic  80.2 us (4%)
  starting transfers between devices  79 us (4%)
  blocking collectives  39.9 us (2%)
    reduce_scatter x3, waiting for transfers between devices, on_device(): lax.psum_scatter(lower_totals + upper_totals, ('dp', 'seq'), scatter_dime...  727 us
    unnamed x9, waiting for transfers between devices  254 us
    dot_general x24, matrix products, weight_term(): lax.dot_general(left, right, (((0,), (0,)), ((), ())), preferred_element_...  132 us
    all_to_all x4, waiting for transfers between devices, on_device(): lax.all_to_all(stacked, 'seq', split_axis=2, concat_axis=3, tiled=True)  78.3 us
    dot_general x24, matrix products, dense(): return jnp.dot(left, right, preferred_element_type=jnp.float32)  77.9 us
    dot_general x24, matrix products, dense_back(): lax.dot_general(left, right, (((1,), (1,)), ((), ())), preferred_element_...  61.9 us
    unnamed x411, local copies, waits for them, and re-layouts  53.2 us
    unnamed x1, blocking collectives  39.9 us
  transfers between devices with their start and end apart: 22, of which 13 were waited for; matrix products, arithmetic and copies ran while one was open for 25% of the time, Pallas kernels for 0%

commit v1 on v0

--- a/solution.py
+++ b/solution.py
@@ -210,9 +210,12 @@
         )
         stacked = jnp.stack([d_queries, d_keys, d_vals]).astype(jnp.bfloat16)
         stacked = stacked.reshape(3, group, slots_all, 1, local_width)
-        returned = lax.all_to_all(stacked, "seq", split_axis=2, concat_axis=3, tiled=True).reshape(
-            3, rows, width
-        )
+        returned = jnp.concatenate(
+            lax.all_to_all(
+                jnp.stack(jnp.split(stacked, lax.axis_size("seq"), axis=2)), "seq", 0, 0
+            ),
+            axis=3,
+        ).reshape(3, rows, width)
         g_w_query = weight_term(block, returned[0])
         g_b_query = jnp.sum(returned[0].astype(jnp.float32), 0)
         g_w_key = weight_term(block, returned[1])

time: 1820 us -> 1770 us (0.973)
  local copies, waits for them, and re-layouts: 188 us -> 152 us
    another operation x28 -> x24, local copies, waits for them, and re-layouts: 41.2 us -> 15.7 us
  transfers between devices with their start and end apart: 22 -> 22, of which waited for: 13 -> 14; matrix products, arithmetic and copies ran while one was open for 25% -> 22% of each run, Pallas kernels for 0% -> 0%
where the time goes in v1:
time: 1770 us; the launch traced here: 1760 us
  waiting for transfers between devices  1090 us (62%)
  matrix products  316 us (18%)
  local copies, waits for them, and re-layouts  152 us (9%)
  starting transfers between devices  79.9 us (5%)
  other arithmetic  64.3 us (4%)
  blocking collectives  43.9 us (2%)
    reduce_scatter x3, waiting for transfers between devices, on_device(): lax.psum_scatter(lower_totals + upper_totals, ('dp', 'seq'), scatter_dime...  727 us
    unnamed x9, waiting for transfers between devices  254 us
    dot_general x24, matrix products, weight_term(): lax.dot_general(left, right, (((0,), (0,)), ((), ())), preferred_element_...  132 us
    all_to_all x4, waiting for transfers between devices, on_device(): lax.all_to_all(jnp.stack(jnp.split(stacked, lax.axis_size('seq'), axis=2)...  85.1 us
    dot_general x24, matrix products, dense(): return jnp.dot(left, right, preferred_element_type=jnp.float32)  78.1 us
    dot_general x24, matrix products, dense_back(): lax.dot_general(left, right, (((1,), (1,)), ((), ())), preferred_element_...  61.7 us
    unnamed x411, local copies, waits for them, and re-layouts  54.3 us
    unnamed x1, blocking collectives  43.9 us
  transfers between devices with their start and end apart: 22, of which 14 were waited for; matrix products, arithmetic and copies ran while one was open for 22% of the time, Pallas kernels for 0%

profile of v1, /device:TPU:0, one launch (start us, length us, event | category | flops | bytes accessed | tf_op | source)
XLA Modules:
  0.0 1762.7 jit_solution(1825769466831503833)
XLA Ops:
  22.5 6.3 all-to-all-start.6
  201.3 5.5 all-to-all-start.3
  212.6 5.4 convolution_add_fusion.3
  218.0 6.3 fusion.296
  240.8 5.6 fusion.293
  263.8 9.7 fusion.302
  283.9 9.4 fusion.299
  298.0 7.4 convert_reduce_fusion.3
  305.5 7.5 convert_reduce_fusion
  313.8 8.1 convert_reduce_fusion.1
  324.8 7.2 convert_reduce_fusion.2
  373.3 7.4 add_add_fusion.2
  446.1 21.8 %all-to-all-done.9 = bf16[4,3,1,128,1,256]{3,5,1,4,2,0:T(8,128)(2,1)} async-done(((bf16[4,3,1,128,1,256]{3,5,1,4,2,0:T(8,128)(2,1)}), bf16[4,3,1,128,1,256]{3,5,1,4,2,0:T(8,128)(2,1)}, u32[]{:S(2)}, u32[]{:S(2)}) %all-to-all-start.9) | async-done | bytes 786464 | tf_op jit(solution)/shard_map/all_to_all | solution.py:214
  478.2 23.6 %all-to-all-done.13 = bf16[4,3,1,128,1,256]{3,5,1,4,2,0:T(8,128)(2,1)} async-done(((bf16[4,3,1,128,1,256]{3,5,1,4,2,0:T(8,128)(2,1)}), bf16[4,3,1,128,1,256]{3,5,1,4,2,0:T(8,128)(2,1)}, u32[]{:S(2)}, u32[]{:S(2)}) %all-to-all-start.13) | async-done | bytes 786464 | tf_op jit(solution)/shard_map/all_to_all | solution.py:214
  501.8 7.7 all-to-all-start.15
  514.7 26.8 %all-to-all-done.15 = bf16[4,3,1,128,1,256]{3,5,1,4,2,0:T(8,128)(2,1)} async-done(((bf16[4,3,1,128,1,256]{3,5,1,4,2,0:T(8,128)(2,1)}), bf16[4,3,1,128,1,256]{3,5,1,4,2,0:T(8,128)(2,1)}, u32[]{:S(2)}, u32[]{:S(2)}) %all-to-all-start.15) | async-done | bytes 786464 | tf_op jit(solution)/shard_map/all_to_all | solution.py:214
  550.5 13.0 all-to-all-done.11
  580.0 5.4 copy.273
  590.8 5.4 copy.271
  597.9 9.7 fusion.252
  607.6 9.8 fusion.246
  617.4 9.7 fusion.240
  627.1 24.0 %add_add_fusion = f32[4096,1024]{1,0:T(8,128)} fusion(f32[4096,1024]{1,0:T(8,128)} %fusion.240, f32[4096,1024]{1,0:T(8,128)} %fusion.252, f32[4096,1024]{1,0:T(8,128)} %fusion.246, f32[128,1024]{1,0:T(8,128)S(1)} %copy-done.38, f32[128,4096]{1,0:T(8,128)S(1)} %copy-done.26), kind=kOutput, calls=%fused_computation | convolution fusion | flops 1120534528 | bytes 69730304 | tf_op jit(solution)/shard_map/dot_general | solution.py:23
  652.2 9.4 fusion.257
  661.7 8.2 fusion.260
  669.9 8.2 fusion.263
  678.1 23.2 %add_add_fusion.1 = f32[1024,4096]{1,0:T(8,128)} fusion(f32[1024,4096]{1,0:T(8,128)} %fusion.257, f32[1024,4096]{1,0:T(8,128)} %fusion.263, f32[1024,4096]{1,0:T(8,128)} %fusion.260, bf16[128,4096]{1,0:T(8,128)(2,1)S(1)} %copy-done.47, f32[128,1024]{1,0:T(8,128)S(1)} %copy-done.15, f32[128]{0:T(128)S(1)} %copy-done.181, f32[128]{0:T(128)S(1)} %copy-done.149, ...), kind=kOutput, calls=%fused_computation.1 | convolution fusion | flops 1086980096 | bytes 68690944 | tf_op jit(solution)/shard_map/dot_general | solution.py:23
  710.5 43.9 %all-reduce.9 = (f32[1024]{0:T(1024)S(1)}, f32[1024]{0:T(1024)S(1)}, f32[1024]{0:T(1024)S(1)}, f32[1024]{0:T(1024)S(1)}, f32[1024]{0:T(1024)S(1)}, /*index=5*/f3...) all-reduce(f32[1024]{0:T(1024)S(1)} %bitcast.541, ...), channel_id=3, replica_groups=mesh['dp'=8,'seq'=4] {'dp','seq'}, use_global_device_ids=true, to_apply=%region_49.50.clone | all-reduce | flops 12288 | bytes 98304
  774.5 103.2 %reduce-scatter.21.cloned.1.call-done = f32[32,1024]{1,0:T(8,128)} async-done(((f32[1024,1024]{1,0:T(8,128)}), f32[32,1024]{1,0:T(8,128)}) %reduce-scatter.21.cloned.1.call-update) | async-done | bytes 131088
  877.7 150.5 %reduce-scatter.19.cloned.1.call-done = f32[32,1024]{1,0:T(8,128)} async-done(((f32[1024,1024]{1,0:T(8,128)}), f32[32,1024]{1,0:T(8,128)}) %reduce-scatter.19.cloned.1.call-update) | async-done | bytes 131088
  1028.2 362.5 %reduce-scatter.17.cloned.1.call-done = f32[128,1024]{1,0:T(8,128)} async-done(((f32[4096,1024]{1,0:T(8,128)}), f32[128,1024]{1,0:T(8,128)}) %reduce-scatter.17.cloned.1.call-update) | async-done | bytes 524304 | tf_op jit(solution)/shard_map/reduce_scatter | solution.py:234
  1390.7 364.7 %reduce-scatter.15.cloned.1.call-done = f32[32,4096]{1,0:T(8,128)} async-done(((f32[1024,4096]{1,0:T(8,128)}), f32[32,4096]{1,0:T(8,128)}) %reduce-scatter.15.cloned.1.call-update) | async-done | bytes 524304 | tf_op jit(solution)/shard_map/reduce_scatter | solution.py:234
  (710 shorter events, 428.6 us)
Async XLA Ops:
  7.2 204.5 %copy-start = (bf16[1024,1024]{1,0:T(8,128)(2,1)S(1)}, bf16[1024,1024]{1,0:T(8,128)(2,1)}, u32[]{:S(2)}) copy-start(bf16[1024,1024]{1,0:T(8,128)(2,1)} %param.26) | copy-start | bytes 6291460
  22.5 26.6 %all-to-all-start.6 = ((bf16[3,1,128,4,256]{4,2,1,0,3:T(8,128)(2,1)}), bf16[3,1,128,4,256]{4,2,1,0,3:T(8,128)(2,1)}, u32[]{:S(2)}, u32[]{:S(2)}) async-start(bf16[3,1,128,4,256]{4,2,1,0,3:T(8,128)(2,1)} %pad_maximum_fusion.5), calls=%async_computation.6 | async-start | bytes 1572864 | tf_op jit(solution)/shard_map/all_to_all | solution.py:110
  49.1 24.0 %all-to-all-start.4 = ((bf16[3,1,128,4,256]{4,2,1,0,3:T(8,128)(2,1)}), bf16[3,1,128,4,256]{4,2,1,0,3:T(8,128)(2,1)}, u32[]{:S(2)}, u32[]{:S(2)}) async-start(bf16[3,1,128,4,256]{4,2,1,0,3:T(8,128)(2,1)} %pad_maximum_fusion.4), calls=%async_computation.4 | async-start | bytes 1572864 | tf_op jit(solution)/shard_map/all_to_all | solution.py:110
  73.0 23.9 %all-to-all-start.2 = ((bf16[3,1,128,4,256]{4,2,1,0,3:T(8,128)(2,1)}), bf16[3,1,128,4,256]{4,2,1,0,3:T(8,128)(2,1)}, u32[]{:S(2)}, u32[]{:S(2)}) async-start(bf16[3,1,128,4,256]{4,2,1,0,3:T(8,128)(2,1)} %pad_maximum_fusion.3), calls=%async_computation.2 | async-start | bytes 1572864 | tf_op jit(solution)/shard_map/all_to_all | solution.py:110
  97.0 35.7 %all-to-all-start = ((bf16[3,1,128,4,256]{4,2,1,0,3:T(8,128)(2,1)}), bf16[3,1,128,4,256]{4,2,1,0,3:T(8,128)(2,1)}, u32[]{:S(2)}, u32[]{:S(2)}) async-start(bf16[3,1,128,4,256]{4,2,1,0,3:T(8,128)(2,1)} %pad_maximum_fusion.2), calls=%async_computation | async-start | bytes 1572864 | tf_op jit(solution)/shard_map/all_to_all | solution.py:110
  158.9 42.4 %all-to-all-start.1 = ((bf16[4,2,16384]{2,1,0:T(2,128)(2,1)}), bf16[4,2,16384]{2,1,0:T(2,128)(2,1)}, u32[]{:S(2)}, u32[]{:S(2)}) async-start(bf16[4,2,16384]{2,1,0:T(2,128)(2,1)} %reshape.1159), calls=%async_computation.1 | async-start | bytes 524288 | tf_op jit(solution)/shard_map/all_to_all | solution.py:132
  201.3 23.1 %all-to-all-start.3 = ((bf16[4,2,16384]{2,1,0:T(2,128)(2,1)}), bf16[4,2,16384]{2,1,0:T(2,128)(2,1)}, u32[]{:S(2)}, u32[]{:S(2)}) async-start(bf16[4,2,16384]{2,1,0:T(2,128)(2,1)} %reshape.1157), calls=%async_computation.3 | async-start | bytes 524288 | tf_op jit(solution)/shard_map/all_to_all | solution.py:132
  212.3 126.4 %copy-start.142 = (f32[128]{0:T(128)}, f32[128]{0:T(128)S(1)}, u32[]{:S(2)}) copy-start(f32[128]{0:T(128)S(1)} %broadcast_multiply_fusion.23) | copy-start | bytes 1540
  212.5 126.2 %copy-start.150 = (f32[128]{0:T(128)}, f32[128]{0:T(128)S(1)}, u32[]{:S(2)}) copy-start(f32[128]{0:T(128)S(1)} %add_rsqrt_fusion.7) | copy-start | bytes 1540
  224.4 23.7 %all-to-all-start.5 = ((bf16[4,2,16384]{2,1,0:T(2,128)(2,1)}), bf16[4,2,16384]{2,1,0:T(2,128)(2,1)}, u32[]{:S(2)}, u32[]{:S(2)}) async-start(bf16[4,2,16384]{2,1,0:T(2,128)(2,1)} %reshape.1155), calls=%async_computation.5 | async-start | bytes 524288 | tf_op jit(solution)/shard_map/all_to_all | solution.py:132
  235.1 111.6 %copy-start.144 = (f32[128]{0:T(128)}, f32[128]{0:T(128)S(1)}, u32[]{:S(2)}) copy-start(f32[128]{0:T(128)S(1)} %broadcast_multiply_fusion.21) | copy-start | bytes 1540
  235.3 111.4 %copy-start.152 = (f32[128]{0:T(128)}, f32[128]{0:T(128)S(1)}, u32[]{:S(2)}) copy-start(f32[128]{0:T(128)S(1)} %add_rsqrt_fusion.5) | copy-start | bytes 1540
  248.1 25.4 %all-to-all-start.7 = ((bf16[4,2,16384]{2,1,0:T(2,128)(2,1)}), bf16[4,2,16384]{2,1,0:T(2,128)(2,1)}, u32[]{:S(2)}, u32[]{:S(2)}) async-start(bf16[4,2,16384]{2,1,0:T(2,128)(2,1)} %reshape.1153), calls=%async_computation.7 | async-start | bytes 524288 | tf_op jit(solution)/shard_map/all_to_all | solution.py:132
  258.8 87.9 %copy-start.146 = (f32[128]{0:T(128)}, f32[128]{0:T(128)S(1)}, u32[]{:S(2)}) copy-start(f32[128]{0:T(128)S(1)} %broadcast_multiply_fusion.19) | copy-start | bytes 1540
  259.0 87.7 %copy-start.154 = (f32[128]{0:T(128)}, f32[128]{0:T(128)S(1)}, u32[]{:S(2)}) copy-start(f32[128]{0:T(128)S(1)} %add_rsqrt_fusion.3) | copy-start | bytes 1540
  278.8 67.9 %copy-start.14 = (f32[128,1024]{1,0:T(8,128)}, f32[128,1024]{1,0:T(8,128)S(1)}, u32[]{:S(2)}) copy-start(f32[128,1024]{1,0:T(8,128)S(1)} %get-tuple-element.249) | copy-start | bytes 1572868
  278.9 67.9 %copy-start.148 = (f32[128]{0:T(128)}, f32[128]{0:T(128)S(1)}, u32[]{:S(2)}) copy-start(f32[128]{0:T(128)S(1)} %broadcast_multiply_fusion.17) | copy-start | bytes 1540
  368.2 12.5 all-to-all-start.8
  373.3 401.3 %reduce-scatter.13.cloned.1.call-start = ((), (), s32[]{:S(2)}) async-start(), calls=%async_computation.22 | async-start | bytes 4325376 | tf_op jit(solution)/shard_map/reduce_scatter | solution.py:234
  380.7 15.5 all-to-all-start.12
  396.2 16.4 all-to-all-start.10
  412.6 15.6 all-to-all-start.14
  431.9 36.0 %all-to-all-start.9 = ((bf16[4,3,1,128,1,256]{3,5,1,4,2,0:T(8,128)(2,1)}), bf16[4,3,1,128,1,256]{3,5,1,4,2,0:T(8,128)(2,1)}, u32[]{:S(2)}, u32[]{:S(2)}) async-start(bf16[4,3,1,128,1,256]{3,5,1,4,2,0:T(8,128)(2,1)} %pad_maximum_fusion.7), calls=%async_computation.9 | async-start | bytes 1572864 | tf_op jit(solution)/shard_map/all_to_all | solution.py:214
  467.8 34.0 %all-to-all-start.13 = ((bf16[4,3,1,128,1,256]{3,5,1,4,2,0:T(8,128)(2,1)}), bf16[4,3,1,128,1,256]{3,5,1,4,2,0:T(8,128)(2,1)}, u32[]{:S(2)}, u32[]{:S(2)}) async-start(bf16[4,3,1,128,1,256]{3,5,1,4,2,0:T(8,128)(2,1)} %pad_maximum_fusion.11), calls=%async_computation.13 | async-start | bytes 1572864 | tf_op jit(solution)/shard_map/all_to_all | solution.py:214
  501.8 39.7 %all-to-all-start.15 = ((bf16[4,3,1,128,1,256]{3,5,1,4,2,0:T(8,128)(2,1)}), bf16[4,3,1,128,1,256]{3,5,1,4,2,0:T(8,128)(2,1)}, u32[]{:S(2)}, u32[]{:S(2)}) async-start(bf16[4,3,1,128,1,256]{3,5,1,4,2,0:T(8,128)(2,1)} %pad_maximum_fusion.13), calls=%async_computation.15 | async-start | bytes 1572864 | tf_op jit(solution)/shard_map/all_to_all | solution.py:214
  541.5 21.9 %all-to-all-start.11 = ((bf16[4,3,1,128,1,256]{3,5,1,4,2,0:T(8,128)(2,1)}), bf16[4,3,1,128,1,256]{3,5,1,4,2,0:T(8,128)(2,1)S(1)}, u32[]{:S(2)}, u32[]{:S(2)}) async-start(bf16[4,3,1,128,1,256]{3,5,1,4,2,0:T(8,128)(2,1)} %pad_maximum_fusion.9), calls=%async_computation.11 | async-start | bytes 1572864 | tf_op jit(solution)/shard_map/all_to_all | solution.py:214
  545.2 229.3 %reduce-scatter.23.cloned.1.call-start = ((), (), s32[]{:S(2)}) async-start(), calls=%async_computation.27 | async-start | bytes 4325376
  574.4 303.3 %reduce-scatter.21.cloned.1.call-start = ((), (), s32[]{:S(2)}) async-start(), calls=%async_computation.26 | async-start | bytes 4325376
  585.4 442.8 %reduce-scatter.19.cloned.1.call-start = ((), (), s32[]{:S(2)}) async-start(), calls=%async_computation.25 | async-start | bytes 4325376
  596.2 794.5 %reduce-scatter.17.cloned.1.call-start = ((), (), s32[]{:S(2)}) async-start(), calls=%async_computation.24 | async-start | bytes 17301504 | tf_op jit(solution)/shard_map/reduce_scatter | solution.py:234
  651.3 1104.2 %reduce-scatter.15.cloned.1.call-start = ((), (), s32[]{:S(2)}) async-start(), calls=%async_computation.23 | async-start | bytes 17301504 | tf_op jit(solution)/shard_map/reduce_scatter | solution.py:234
  772.1 983.4 %copy-start.1 = (bf16[1024,1024]{1,0:T(8,128)(2,1)S(1)}, bf16[1024,1024]{1,0:T(8,128)(2,1)}, u32[]{:S(2)}) copy-start(bf16[1024,1024]{1,0:T(8,128)(2,1)} %param.26) | copy-start | bytes 6291460
  (182 other events, 1483.7 us)
Sparse Core Ops, SparseCore 0:
  380.8 168.8 reduce-scatter.12
  574.5 151.9 reduce-scatter.22
  729.4 148.3 reduce-scatter.20
  880.4 147.7 reduce-scatter.18
  1030.9 359.7 reduce-scatter.16
  1393.5 361.9 reduce-scatter.14
